TPU v7x, 512 devices: a whole 4x8x8 slice. The times are simulated.
512 devices in a mesh: cfg: 2 (over core), req: 2 (over y_lo), seq: 128 (over z, x, y_hi).
Axes of the slice: x: 4, y: 8 (y_hi: 4, y_lo: 2; y = y_hi * 2 + y_lo), z: 8, core: 2. Of those that a mesh axis runs over, the one named last changes fastest.
Arguments:
- q_image: bfloat16 [2, 2048, 2048], P('cfg', ('req', 'seq')), parts along dimension 1, may hold values from -8 to 8
- k_image: bfloat16 [2, 2048, 2048], P('cfg', ('req', 'seq')), parts along dimension 1, may hold values from -8 to 8
- v_image: bfloat16 [2, 2048, 2048], P('cfg', ('req', 'seq')), parts along dimension 1, may hold values from -5 to 5
- k_text: bfloat16 [2, 1024, 2048], P('cfg', ('req', 'seq')), parts along dimension 1, may hold values from -6 to 6
- v_text: bfloat16 [2, 1024, 2048], P('cfg', ('req', 'seq')), parts along dimension 1, may hold values from -5 to 5
- text_len: int32 [2, 2], P('cfg', 'req'), parts along dimension 1, may hold values from 1 to 512
- shift: float32 [2, 2, 2048], P('cfg', 'req'), parts along dimension 1, may hold values from -1.5 to 1.5
- scale: float32 [2, 2, 2048], P('cfg', 'req'), parts along dimension 1, may hold values from -1.5 to 1.5
- w_latent: bfloat16 [2048, 64], replicated, may hold values from -0.125 to 0.125
- latents: float32 [2048, 64], P(('req', 'seq')), parts along dimension 0, may hold values from -1.2 to 1.2
- step_index: int32 [1], replicated, may hold values from 22 to 27
Outputs:
- latents_next: float32 [2048, 64], P(('req', 'seq'), 'cfg'), parts along dimension 0
- guided: float32 [2048, 64], P(('req', 'seq'), 'cfg'), parts along dimension 0
- norm: float32 [2], P('req'), parts along dimension 0
- max_logit: float32 [2, 2, 16], P('cfg', 'req'), parts along dimension 1
There are 2 independent parts, one for each index of `req`. A program takes and returns all parts, laid end to end along the dimension named above; an argument that names none is the same for every part. Nothing has to cross between parts.
All inputs are finite; a program needn't handle non-finite values.
Results may differ from a plain program's by a relative error of at most 0.0062.
Values may be sent and summed in bfloat16 or wider, within the bound.
A program may use at most 64 MiB of HBM per device.

v0:
```python
import math

import jax
import jax.numpy as jnp
from jax import lax
from jax.sharding import PartitionSpec as P

HEADS = 16
HEAD_DIM = 128
CHAN = 64
STEPS = 28


GUIDANCE = 3.5
SIGMA_SHIFT = 3.0


def partner(value, axis, bit):
    mask = 2**bit
    pairs = [(source, source ^ mask) for source in range(lax.axis_size(axis))]
    return lax.ppermute(value, axis, pairs)


def sigma_at(position):
    level = 1.0 - position.astype(jnp.float32) / STEPS
    return SIGMA_SHIFT * level / (1.0 + (SIGMA_SHIFT - 1.0) * level)


def scores_of(queries, key_block, inv_root):
    return (
        jnp.einsum("qhd,khd->hqk", queries, key_block, preferred_element_type=jnp.float32)
        * inv_root
    )


def attend(queries, image_keys, image_values, text_keys, text_values, length):
    row_count, head_count, head_width = queries.shape
    text_rows = text_keys.shape[0]
    inv_root = 1.0 / math.sqrt(head_width)
    query_span = min(128, row_count)
    query_blocks = row_count // query_span

    def one_block(query_block):
        image_scores = scores_of(query_block, image_keys, inv_root)
        row_peak = jnp.max(image_scores, axis=-1)
        position = lax.iota(jnp.int32, text_rows)
        text_scores = jnp.where(
            (position < length)[None, None, :],
            scores_of(query_block, text_keys, inv_root),
            -jnp.inf,
        )
        row_peak = jnp.maximum(row_peak, jnp.max(text_scores, axis=-1))

        def absorb(scores, value_block, running):
            weight_sum, summed = running
            weights = jnp.exp(scores - row_peak[:, :, None]).astype(jnp.bfloat16)
            weight_sum = weight_sum + jnp.sum(weights.astype(jnp.float32), axis=-1)
            summed = summed + jnp.einsum(
                "hqk,khd->qhd", weights, value_block, preferred_element_type=jnp.float32
            )
            return (weight_sum, summed)

        running = (
            jnp.zeros((head_count, query_span), jnp.float32),
            jnp.zeros((query_span, head_count, head_width), jnp.float32),
        )
        running = absorb(image_scores, image_values, running)
        running = absorb(text_scores, text_values, running)
        weight_sum, summed = running
        attended = (summed / jnp.transpose(weight_sum)[:, :, None]).astype(jnp.bfloat16)
        return (attended.reshape(query_span, head_count * head_width), jnp.max(row_peak, axis=1))

    outputs, maxima = lax.map(
        one_block, queries.reshape(query_blocks, query_span, head_count, head_width)
    )
    return (outputs.reshape(row_count, head_count * head_width), jnp.max(maxima, axis=0))


def spread_copies(matrix, qparts, groups, span_dev):
    row_count = matrix.shape[0]
    repeated = jnp.broadcast_to(
        matrix.reshape(row_count, 1, groups, span_dev), (row_count, qparts, groups, span_dev)
    )
    return repeated.reshape(row_count, qparts * groups, span_dev)


def per_device(
    q_image, k_image, v_image, k_text, v_text, text_len, shift, scale, w_latent, latents, step_index
):
    devices = lax.axis_size("seq")
    tokens = q_image.shape[1]
    features = q_image.shape[2]
    qparts = max(1, devices // HEADS)
    heads_dev = HEADS * qparts // devices
    groups = HEADS // heads_dev
    span_dev = heads_dev * HEAD_DIM
    part_rows = tokens // qparts
    queries = lax.all_to_all(
        q_image[0].reshape(part_rows, devices, span_dev),
        "seq",
        split_axis=1,
        concat_axis=1,
        tiled=True,
    )
    queries = queries.reshape(part_rows * devices, heads_dev, HEAD_DIM)
    text_k_spread = spread_copies(k_text[0], qparts, groups, span_dev)
    text_v_spread = spread_copies(v_text[0], qparts, groups, span_dev)
    image_keys, image_values, text_keys, text_values = (
        lax.all_to_all(
            spread_copies(k_image[0], qparts, groups, span_dev),
            "seq",
            split_axis=1,
            concat_axis=0,
            tiled=True,
        ),
        lax.all_to_all(
            spread_copies(v_image[0], qparts, groups, span_dev),
            "seq",
            split_axis=1,
            concat_axis=0,
            tiled=True,
        ),
        lax.all_to_all(text_k_spread, "seq", split_axis=1, concat_axis=0, tiled=True),
        lax.all_to_all(text_v_spread, "seq", split_axis=1, concat_axis=0, tiled=True),
    )
    length = text_len[0, 0]
    attended, head_peak = attend(queries, image_keys, image_values, text_keys, text_values, length)
    returned = lax.all_to_all(
        attended.reshape(part_rows, devices, span_dev),
        "seq",
        split_axis=1,
        concat_axis=1,
        tiled=True,
    )
    feature_rows = returned.reshape(tokens, features).astype(jnp.float32)
    average = jnp.mean(feature_rows, axis=1, keepdims=True)
    centered = feature_rows - average
    variance = jnp.mean(centered * centered, axis=1, keepdims=True)
    normed = (centered * lax.rsqrt(variance + 1e-06) * (1.0 + scale[0, 0]) + shift[0, 0]).astype(
        jnp.bfloat16
    )
    velocity = jnp.dot(normed, w_latent, preferred_element_type=jnp.float32)
    partner_velocity = partner(velocity, "cfg", 0)
    copy_index = lax.axis_index("cfg")
    cond_velocity = jnp.where(copy_index == 0, velocity, partner_velocity)
    uncond_velocity = jnp.where(copy_index == 0, partner_velocity, velocity)
    guided = uncond_velocity + GUIDANCE * (cond_velocity - uncond_velocity)
    delta = sigma_at(step_index[0] + 1) - sigma_at(step_index[0])
    latents_next = latents + delta * guided
    square_local = jnp.sum(latents_next * latents_next)
    group_index = lax.axis_index("seq") % groups
    peak_full = jnp.full((HEADS,), -jnp.inf, jnp.float32)
    peak_full = lax.dynamic_update_slice_in_dim(peak_full, head_peak, group_index * heads_dev, 0)
    peak_total = lax.pmax(peak_full, "seq")
    square_total = lax.psum(square_local, "seq")
    norm = jnp.sqrt(square_total / (tokens * devices * CHAN)).reshape(1)
    half_cols = CHAN // lax.axis_size("cfg")
    col_start = copy_index * half_cols
    latents_half = lax.dynamic_slice_in_dim(latents_next, col_start, half_cols, 1)
    guided_half = lax.dynamic_slice_in_dim(guided, col_start, half_cols, 1)
    return (latents_half, guided_half, norm, peak_total.reshape(1, 1, HEADS))


def solution(mesh):
    placed = (
        P("cfg", ("req", "seq"), None),
        P("cfg", ("req", "seq"), None),
        P("cfg", ("req", "seq"), None),
        P("cfg", ("req", "seq"), None),
        P("cfg", ("req", "seq"), None),
        P("cfg", "req"),
        P("cfg", "req", None),
        P("cfg", "req", None),
        P(),
        P(("req", "seq"), None),
        P(),
    )
    return jax.shard_map(
        per_device,
        mesh=mesh,
        in_specs=placed,
        out_specs=(
            P(("req", "seq"), "cfg"),
            P(("req", "seq"), "cfg"),
            P("req"),
            P("cfg", "req", None),
        ),
        check_vma=False,
    )
```

profile of v0, /device:TPU:8, one launch (start us, length us, event | category | flops | bytes accessed | tf_op | source)
XLA Modules:
  0.0 899.8 jit_solution(13826981710047733702)
XLA Ops:
  0.6 0.0 copy-start
  0.6 0.8 reshape_squeeze.3
  1.5 0.0 copy-start.3
  1.5 33.5 %all_to_all.70 = bf16[1,128,128]{2,0,1:T(2,128)(2,1)S(1)} all-to-all(bf16[1,128,128]{2,0,1:T(2,128)(2,1)S(1)} %reshape_squeeze.3), channel_id=1, replica_groups=mesh['cfg'=2,'req'=2,'seq'=128] {'seq'}, dimensions={1} | all-to-all | bytes 65536 | tf_op jit(solution)/shard_map/all_to_all | solution.py:98
  35.0 0.0 copy-done.3
  35.0 0.0 copy-start.1
  35.0 20.3 %all_to_all.71 = bf16[4,128,128]{2,0,1:T(4,128)(2,1)S(1)} all-to-all(bf16[4,128,128]{2,0,1:T(4,128)(2,1)S(1)} %bitcast.68), channel_id=1, replica_groups=mesh['cfg'=2,'req'=2,'seq'=128] {'seq'}, dimensions={1} | all-to-all | bytes 262144 | tf_op jit(solution)/shard_map/all_to_all | solution.py:123
  55.3 0.0 copy-done.1
  55.3 0.7 broadcast_in_dim.62
  56.0 6.2 all-to-all-start.1
  62.9 0.0 copy-start.2
  62.9 0.3 fusion.21
  63.1 15.0 %all-to-all-done.1 = bf16[8,128,128]{2,0,1:T(8,128)(2,1)S(1)} async-done(((bf16[8,128,128]{2,0,1:T(8,128)(2,1)}), bf16[8,128,128]{2,0,1:T(8,128)(2,1)S(1)}, u32[]{:S(2)}, u32[]{:S(2)}) %all-to-all-start.1) | async-done | bytes 262176 | tf_op jit(solution)/shard_map/all_to_all | solution.py:109
  78.1 0.0 copy-done.2
  78.1 0.7 broadcast_in_dim.68
  78.8 6.2 all-to-all-start.3
  85.0 0.3 fusion.20
  85.3 0.6 fusion.19
  85.9 0.0 copy-start.4
  85.9 0.2 convert_reduce_fusion
  86.2 14.5 %all-to-all-done.3 = bf16[8,128,128]{2,0,1:T(8,128)(2,1)S(1)} async-done(((bf16[8,128,128]{2,0,1:T(8,128)(2,1)}), bf16[8,128,128]{2,0,1:T(8,128)(2,1)S(1)}, u32[]{:S(2)}, u32[]{:S(2)}) %all-to-all-start.3) | async-done | bytes 262176 | tf_op jit(solution)/shard_map/all_to_all | solution.py:116
  100.7 0.0 copy-done.4
  100.7 0.7 broadcast_in_dim.70
  101.3 6.2 all-to-all-start.4
  107.5 0.2 convert_reduce_fusion.1
  107.7 0.3 fusion.5
  108.0 14.1 %all-to-all-done.4 = bf16[4,128,128]{2,0,1:T(4,128)(2,1)S(1)} async-done(((bf16[4,128,128]{2,0,1:T(4,128)(2,1)}), bf16[4,128,128]{2,0,1:T(4,128)(2,1)S(1)}, u32[]{:S(2)}, u32[]{:S(2)}) %all-to-all-start.4) | async-done | bytes 131104 | tf_op jit(solution)/shard_map/all_to_all | solution.py:124
  122.1 0.2 fusion.4
  122.4 0.7 copy.25
  123.0 0.0 copy-start.5
  123.0 6.5 all-to-all-start.5
  129.5 0.0 copy-done.5
  130.2 13.6 %all-to-all-done.5 = bf16[1,128,128]{2,0,1:T(2,128)(2,1)S(1)} async-done(((bf16[1,128,128]{2,0,1:T(2,128)(2,1)}), bf16[1,128,128]{2,0,1:T(2,128)(2,1)S(1)}, u32[]{:S(2)}, u32[]{:S(2)}) %all-to-all-start.5) | async-done | bytes 32800 | tf_op jit(solution)/shard_map/all_to_all | solution.py:128
  143.8 1.0 convert_reduce_fusion.2
  144.8 0.1 reduce_sum.64
  144.9 0.1 reduce_sum.65
  145.0 0.1 sub.67
  145.1 0.1 sub.68
  145.2 1.9 fusion.9
  147.1 0.0 copy-start.7
  147.1 0.1 reduce_sum.67
  147.2 0.1 reduce_sum.68
  147.3 0.0 copy-done
  147.3 0.5 copy-done.7
  147.8 0.2 fusion.10
  148.0 1.9 collective-permute-start
  150.1 0.0 copy-start.6
  150.1 0.7 dynamic_update_slice.10
  150.8 372.1 %pmax.7 = f32[1,1,16]{2,1,0:T(1,128)} all-reduce(f32[1,1,16]{2,1,0:T(1,128)S(1)} %dynamic_update_slice.10), channel_id=1, replica_groups=mesh['cfg'=2,'req'=2,'seq'=128] {'seq'}, use_global_device_ids=true, to_apply=%region_11.12 | all-reduce | flops 16 | bytes 128 | tf_op jit(solution)/shard_map/pmax | solution.py:154
  522.9 0.0 collective-permute-done
  522.9 0.0 copy-done.6
  522.9 0.6 multiply_reduce_fusion
  523.5 373.7 %psum.7 = f32[]{:T(128)} all-reduce(f32[]{:T(128)} %get-tuple-element.26), channel_id=1, replica_groups=mesh['cfg'=2,'req'=2,'seq'=128] {'seq'}, use_global_device_ids=true, to_apply=%region_9.10 | all-reduce | flops 1 | bytes 8 | tf_op jit(solution)/shard_map/psum | solution.py:155
  898.0 0.7 constant_dynamic-slice_fusion
  (8 shorter events, 0.1 us)
Async XLA Ops:
  0.6 146.7 %copy-start = (bf16[2048,64]{0,1:T(8,128)(2,1)S(1)}, bf16[2048,64]{0,1:T(8,128)(2,1)}, u32[]{:S(2)}) copy-start(bf16[2048,64]{0,1:T(8,128)(2,1)} %param.19) | copy-start | bytes 786436
  1.5 33.5 %copy-start.3 = (bf16[1,4,2048]{2,1,0:T(4,128)(2,1)S(1)}, bf16[1,4,2048]{2,1,0:T(4,128)(2,1)}, u32[]{:S(2)}) copy-start(bf16[1,4,2048]{2,1,0:T(4,128)(2,1)} %param.14) | copy-start | bytes 49156
  35.0 20.3 %copy-start.1 = (bf16[1,8,2048]{2,1,0:T(8,128)(2,1)S(1)}, bf16[1,8,2048]{2,1,0:T(8,128)(2,1)}, u32[]{:S(2)}) copy-start(bf16[1,8,2048]{2,1,0:T(8,128)(2,1)} %param.12) | copy-start | bytes 98308
  56.0 22.1 %all-to-all-start.1 = ((bf16[8,128,128]{2,0,1:T(8,128)(2,1)}), bf16[8,128,128]{2,0,1:T(8,128)(2,1)S(1)}, u32[]{:S(2)}, u32[]{:S(2)}) async-start(bf16[8,128,128]{2,0,1:T(8,128)(2,1)} %bitcast.2), calls=%async_computation.1 | async-start | bytes 524288 | tf_op jit(solution)/shard_map/all_to_all | solution.py:109
  62.9 15.2 %copy-start.2 = (bf16[1,8,2048]{2,1,0:T(8,128)(2,1)S(1)}, bf16[1,8,2048]{2,1,0:T(8,128)(2,1)}, u32[]{:S(2)}) copy-start(bf16[1,8,2048]{2,1,0:T(8,128)(2,1)} %param.13) | copy-start | bytes 98308
  78.8 21.8 %all-to-all-start.3 = ((bf16[8,128,128]{2,0,1:T(8,128)(2,1)}), bf16[8,128,128]{2,0,1:T(8,128)(2,1)S(1)}, u32[]{:S(2)}, u32[]{:S(2)}) async-start(bf16[8,128,128]{2,0,1:T(8,128)(2,1)} %bitcast.13), calls=%async_computation.3 | async-start | bytes 524288 | tf_op jit(solution)/shard_map/all_to_all | solution.py:116
  85.9 14.7 %copy-start.4 = (bf16[1,4,2048]{2,1,0:T(4,128)(2,1)S(1)}, bf16[1,4,2048]{2,1,0:T(4,128)(2,1)}, u32[]{:S(2)}) copy-start(bf16[1,4,2048]{2,1,0:T(4,128)(2,1)} %param.15) | copy-start | bytes 49156
  101.3 20.8 %all-to-all-start.4 = ((bf16[4,128,128]{2,0,1:T(4,128)(2,1)}), bf16[4,128,128]{2,0,1:T(4,128)(2,1)S(1)}, u32[]{:S(2)}, u32[]{:S(2)}) async-start(bf16[4,128,128]{2,0,1:T(4,128)(2,1)} %bitcast.18), calls=%async_computation.4 | async-start | bytes 262144 | tf_op jit(solution)/shard_map/all_to_all | solution.py:124
  123.0 6.5 copy-start.5
  123.0 20.8 %all-to-all-start.5 = ((bf16[1,128,128]{2,0,1:T(2,128)(2,1)}), bf16[1,128,128]{2,0,1:T(2,128)(2,1)S(1)}, u32[]{:S(2)}, u32[]{:S(2)}) async-start(bf16[1,128,128]{2,0,1:T(2,128)(2,1)} %copy.25), calls=%async_computation.5 | async-start | bytes 131072 | tf_op jit(solution)/shard_map/all_to_all | solution.py:128
  147.1 0.7 copy-start.7
  148.0 374.9 %collective-permute-start = (f32[8,64]{1,0:T(8,128)S(1)}, f32[8,64]{1,0:T(8,128)S(1)}, u32[]{:S(2)}, u32[]{:S(2)}) collective-permute-start(f32[8,64]{1,0:T(8,128)S(1)} %fusion.10), channel_id=1, source_target_pairs={{0,256},{256,0},{1,257},{257,1},{2,258},{258,2},{3,259},{259,3},{4... | collective-permute-start | bytes 6152 | tf_op jit(solution)/shard_map/ppermute | solution.py:21
  150.1 372.9 %copy-start.6 = (f32[8,64]{1,0:T(8,128)S(1)}, f32[8,64]{1,0:T(8,128)}, u32[]{:S(2)}) copy-start(f32[8,64]{1,0:T(8,128)} %param.20) | copy-start | bytes 6148
where the time goes:
time: 900 us
  blocking collectives  800 us (89%)
  waiting for transfers between devices  57.1 us (6%)
  starting transfers between devices  26.9 us (3%)
    psum x1, blocking collectives, per_device(): square_total = lax.psum(square_local, 'seq')  374 us
    pmax x1, blocking collectives, per_device(): peak_total = lax.pmax(peak_full, 'seq')  372 us
    all_to_all x1, blocking collectives, per_device(): lax.all_to_all(q_image[0].reshape(part_rows, devices, span_dev), 'seq', s...  33.5 us
    all_to_all x1, blocking collectives, per_device(): lax.all_to_all(text_k_spread, 'seq', split_axis=1, concat_axis=0, tiled=T...  20.3 us
  transfers between devices with their start and end apart: 5, of which 4 were waited for; matrix products, arithmetic and copies ran while one was open for 0% of the time, Pallas kernels for 0%

commit v1 on v0

v1 whole, which is shorter than its diff:
```python
import math

import jax
import jax.numpy as jnp
from jax import lax
from jax.experimental import pallas as pl
from jax.experimental.pallas import tpu as pltpu
from jax.sharding import PartitionSpec as P

HEADS = 16
HEAD_DIM = 128
FEAT = HEADS * HEAD_DIM
CHAN = 64
STEPS = 28
GUIDANCE = 3.5
SIGMA_SHIFT = 3.0

NZ, NX, NY = 8, 4, 4
SEQ = NZ * NX * NY
ROWS = 8
TROWS = 4
OWNERS = NZ * NX
QROWS = OWNERS * ROWS
UNITS = HEADS * NY
FAR_4 = (2, 1, 3, 0)

MESH = pl.DeviceIdType.MESH
BF16 = jnp.bfloat16
F32 = jnp.float32


def remote(src, dst, send_sem, recv_sem, device):
    return pltpu.make_async_remote_copy(
        src_ref=src,
        dst_ref=dst,
        send_sem=send_sem,
        recv_sem=recv_sem,
        device_id=device,
        device_id_type=MESH,
    )


def wait_bytes(ref, sem):
    pltpu.make_async_copy(ref, ref, sem).wait()


def nt_dot(a, b):
    return lax.dot_general(a, b, (((1,), (1,)), ((), ())), preferred_element_type=F32)


def sigma_at(position):
    level = 1.0 - position / STEPS
    return SIGMA_SHIFT * level / (1.0 + (SIGMA_SHIFT - 1.0) * level)


def far_first(i):
    return NZ // 2 + ((i + 1) // 2) * (1 - 2 * lax.rem(i, 2))


def over_z(body):
    def step(i, carry):
        body(far_first(i), False)
        return carry

    lax.fori_loop(0, NZ - 1, step, 0)
    body(0, True)


def kernel(
    len_ref,
    step_ref,
    q_hbm,
    k_hbm,
    v_hbm,
    kt_hbm,
    vt_hbm,
    shift_hbm,
    scale_hbm,
    w_hbm,
    lat_hbm,
    lat_out,
    guided_out,
    norm_out,
    peak_out,
    q_own,
    k_own,
    v_own,
    kt_own,
    vt_own,
    w_own,
    lat_own,
    mod,
    q_send,
    k_send,
    t_send,
    v_send,
    q_all,
    k_all,
    t_all,
    v_all,
    att,
    peak_row,
    heads_in,
    sums,
    local_sem,
    send_sem,
    recv_sem,
):
    cfg = lax.axis_index("cfg")
    me = lax.axis_index("seq")
    other = 1 - cfg
    z = me // (NX * NY)
    x = lax.rem(me // NY, NX)
    y = lax.rem(me, NY)
    attends = lax.rem(z + x, 2) == cfg
    idle = lax.rem(z + x, 2) != cfg
    my_head = z * 2 + x // 2
    my_slot = z * NX + x
    xs = [lax.rem(x + d, NX) for d in FAR_4]
    ys = [lax.rem(y + d, NY) for d in FAR_4]
    plane = [xx * NY + yy for xx in xs for yy in ys]

    loads = [
        (q_hbm.at[0], q_own),
        (k_hbm.at[0], k_own),
        (kt_hbm.at[0], kt_own),
        (vt_hbm.at[0], vt_own),
        (v_hbm.at[0], v_own),
        (shift_hbm.at[0], mod.at[cfg, 0]),
        (scale_hbm.at[0], mod.at[cfg, 1]),
        (w_hbm, w_own),
        (lat_hbm, lat_own),
    ]
    copies = [pltpu.make_async_copy(s, d, local_sem.at[i]) for i, (s, d) in enumerate(loads)]
    for copy in copies:
        copy.start()

    barrier = pltpu.get_barrier_semaphore()

    def greet(device):
        pl.semaphore_signal(barrier, inc=1, device_id=device, device_id_type=MESH)

    greet({"cfg": other, "seq": me})

    @pl.when(attends)
    def _():
        def signals(dz, here):
            base = lax.rem(z + dz, NZ) * (NX * NY)
            for offset in plane[:-1] if here else plane:
                greet({"cfg": cfg, "seq": base + offset})

        over_z(signals)

    for copy in copies:
        copy.wait()
    for h in range(HEADS):
        cols = slice(h * HEAD_DIM, (h + 1) * HEAD_DIM)
        q_send[h] = q_own[:, cols]
        k_send[h] = k_own[:, cols]
        t_send[h, 0] = kt_own[:, cols]
        t_send[h, 1] = vt_own[:, cols]
        v_send[h] = v_own[:, cols]

    @pl.when(attends)
    def _():
        pl.semaphore_wait(barrier, UNITS)

    @pl.when(idle)
    def _():
        pl.semaphore_wait(barrier, UNITS + 1)

    def to_units(pieces):
        def sends(dz, here):
            zz = lax.rem(z + dz, NZ)
            parity = lax.rem(zz + cfg, 2)
            base = (zz * NX + parity) * NY
            for dy, yy in zip(FAR_4, ys):
                for half in range(2):
                    head = zz * 2 + half
                    unit = base + (2 * half * NY + yy)

                    def away():
                        for i, src, dst in pieces(head, dy == 0):
                            device = {"cfg": cfg, "seq": unit}
                            remote(src, dst, send_sem.at[i], recv_sem.at[i], device).start()

                    def local():
                        for i, src, dst in pieces(head, True):
                            pltpu.make_async_copy(src, dst, recv_sem.at[i]).start()

                    if here and dy == 0:
                        pl.when(2 * half + parity != x)(away)
                        pl.when(2 * half + parity == x)(local)
                    else:
                        away()

        over_z(sends)

    def keys(head, own_block):
        parts = [(0, k_send.at[head], k_all.at[me]), (1, t_send.at[head], t_all.at[me])]
        if own_block:
            parts.append((2, q_send.at[head], q_all.at[my_slot]))
        return parts

    to_units(keys)
    to_units(lambda head, own_block: [(3, v_send.at[head], v_all.at[me])])

    mod_copy = remote(
        mod.at[cfg], mod.at[cfg], send_sem.at[4], recv_sem.at[4], {"cfg": other, "seq": me}
    )
    mod_copy.start()
    lane = lax.broadcasted_iota(jnp.int32, (1, HEAD_DIM), 1)
    peak_row[...] = jnp.full((1, HEAD_DIM), -jnp.inf)

    @pl.when(attends)
    def _():
        wait_bytes(k_all, recv_sem.at[0])
        wait_bytes(t_all, recv_sem.at[1])
        wait_bytes(q_all, recv_sem.at[2])
        inv_root = 1.0 / math.sqrt(HEAD_DIM)
        rate = inv_root * math.log2(math.e)
        q = q_all[...].reshape(QROWS, HEAD_DIM)
        image = nt_dot(q, k_all[...].reshape(SEQ * ROWS, HEAD_DIM))
        text = nt_dot(q, t_all[:, 0].reshape(SEQ * TROWS, HEAD_DIM))
        position = lax.broadcasted_iota(jnp.int32, (1, SEQ * TROWS), 1)
        text = jnp.where(position < len_ref[...], text, -jnp.inf)
        peak = jnp.maximum(
            jnp.max(image, axis=1, keepdims=True), jnp.max(text, axis=1, keepdims=True)
        )
        image = jnp.exp2((image - peak) * rate).astype(BF16)
        text = jnp.exp2((text - peak) * rate).astype(BF16)
        top = jnp.max(peak, axis=0, keepdims=True) * inv_root
        peak_row[...] = jnp.where(lane == my_head, top, -jnp.inf)
        wait_bytes(v_all, recv_sem.at[3])
        ones = jnp.ones((SEQ * ROWS, HEAD_DIM), BF16)
        v_image = jnp.concatenate([v_all[...].reshape(SEQ * ROWS, HEAD_DIM), ones], axis=1)
        v_text = jnp.concatenate(
            [t_all[:, 1].reshape(SEQ * TROWS, HEAD_DIM), ones[: SEQ * TROWS]], axis=1
        )
        summed = jnp.dot(image, v_image, preferred_element_type=F32) + jnp.dot(
            text, v_text, preferred_element_type=F32
        )
        result = (summed[:, :HEAD_DIM] / summed[:, HEAD_DIM:]).astype(BF16)
        att[...] = result.reshape(OWNERS, ROWS, HEAD_DIM)

        def give(dz, here):
            base = lax.rem(z + dz, NZ) * NX
            for dx, xx in zip(FAR_4, xs):
                slot = base + xx
                dst = heads_in.at[cfg, my_head]
                owner = slot * NY + y
                remote(
                    att.at[slot], dst, send_sem.at[5], recv_sem.at[5], {"cfg": other, "seq": owner}
                ).start()
                if here and dx == 0:
                    pltpu.make_async_copy(att.at[slot], dst, recv_sem.at[5]).start()
                else:
                    remote(
                        att.at[slot], dst, send_sem.at[5], recv_sem.at[5], {"cfg": cfg, "seq": owner}
                    ).start()

        over_z(give)

    mod_copy.wait_recv()
    wait_bytes(heads_in, recv_sem.at[5])
    parts = heads_in[...].astype(F32)
    average = jnp.sum(jnp.sum(parts, axis=1, keepdims=True), axis=3, keepdims=True) / FEAT
    parts = parts - average
    squares = jnp.sum(parts * parts, axis=1, keepdims=True)
    variance = jnp.sum(squares, axis=3, keepdims=True) / FEAT
    factor = lax.rsqrt(variance + 1e-06)
    normed = (parts * factor * (1.0 + mod[:, 1]) + mod[:, 0]).astype(BF16)
    normed = jnp.concatenate([normed[:, h] for h in range(HEADS)], axis=2)
    velocity = nt_dot(normed.reshape(2 * ROWS, FEAT), w_own[...])
    uncond = velocity[ROWS:]
    guided = uncond + GUIDANCE * (velocity[:ROWS] - uncond)
    position = jnp.broadcast_to(step_ref[...].astype(F32), (1, CHAN))
    delta = sigma_at(position + 1.0) - sigma_at(position)
    latents = lat_own[...] + delta * guided
    square = jnp.sum(
        jnp.sum(latents * latents, axis=1, keepdims=True), axis=0, keepdims=True
    )
    sums[me] = jnp.where(lane == HEADS, square, peak_row[...])

    def share(dz, here):
        base = lax.rem(z + dz, NZ) * (NX * NY)
        for offset in plane[:-1] if here else plane:
            remote(
                sums.at[me],
                sums.at[me],
                send_sem.at[6],
                recv_sem.at[6],
                {"cfg": cfg, "seq": base + offset},
            ).start()

    over_z(share)

    half = CHAN // 2
    lat_out[...] = jnp.where(cfg == 0, latents[:, :half], latents[:, half:])
    guided_out[...] = jnp.where(cfg == 0, guided[:, :half], guided[:, half:])

    mod_copy.wait_send()

    @pl.when(attends)
    def _():
        wait_bytes(k_all.at[: UNITS - 1], send_sem.at[0])
        wait_bytes(t_all.at[: UNITS - 1], send_sem.at[1])
        wait_bytes(q_all.at[: HEADS - 1], send_sem.at[2])
        wait_bytes(v_all.at[: UNITS - 1], send_sem.at[3])
        wait_bytes(k_all.at[: 2 * OWNERS - 1], send_sem.at[5])

    @pl.when(idle)
    def _():
        wait_bytes(k_all.at[:UNITS], send_sem.at[0])
        wait_bytes(t_all.at[:UNITS], send_sem.at[1])
        wait_bytes(q_all.at[:HEADS], send_sem.at[2])
        wait_bytes(v_all.at[:UNITS], send_sem.at[3])

    wait_bytes(sums.at[: SEQ - 1], recv_sem.at[6])
    wait_bytes(sums.at[: SEQ - 1], send_sem.at[6])
    rows = sums[...]
    norm = jnp.sqrt(jnp.sum(rows, axis=0) / (SEQ * ROWS * CHAN))
    norm_out[...] = norm[:, HEADS : HEADS + 1]
    peak_out[...] = jnp.max(rows, axis=0)[:, :HEADS]


def hand_over(*refs):
    sem = refs[8]
    copies = [pltpu.make_async_copy(refs[i], refs[4 + i], sem.at[i]) for i in range(4)]
    for copy in copies:
        copy.start()
    for copy in copies:
        copy.wait()


def per_device(
    q_image, k_image, v_image, k_text, v_text, text_len, shift, scale, w_latent, latents, step_index
):
    anywhere = pl.BlockSpec(memory_space=pltpu.HBM)
    vmem = pl.BlockSpec(memory_space=pltpu.VMEM)
    half = CHAN // 2
    shapes = [
        jax.ShapeDtypeStruct((ROWS, half), F32),
        jax.ShapeDtypeStruct((ROWS, half), F32),
        jax.ShapeDtypeStruct((1, 1), F32),
        jax.ShapeDtypeStruct((1, HEADS), F32),
    ]
    results = pl.pallas_call(
        kernel,
        out_shape=shapes,
        in_specs=[vmem] * 2 + [anywhere] * 9,
        out_specs=[vmem] * 4,
        scratch_shapes=[
            pltpu.VMEM((ROWS, FEAT), BF16),
            pltpu.VMEM((ROWS, FEAT), BF16),
            pltpu.VMEM((ROWS, FEAT), BF16),
            pltpu.VMEM((TROWS, FEAT), BF16),
            pltpu.VMEM((TROWS, FEAT), BF16),
            pltpu.VMEM((CHAN, FEAT), BF16),
            pltpu.VMEM((ROWS, CHAN), F32),
            pltpu.VMEM((2, 2, HEADS, 1, HEAD_DIM), F32),
            pltpu.VMEM((HEADS, ROWS, HEAD_DIM), BF16),
            pltpu.VMEM((HEADS, ROWS, HEAD_DIM), BF16),
            pltpu.VMEM((HEADS, 2, TROWS, HEAD_DIM), BF16),
            pltpu.VMEM((HEADS, ROWS, HEAD_DIM), BF16),
            pltpu.VMEM((OWNERS, ROWS, HEAD_DIM), BF16),
            pltpu.VMEM((SEQ, ROWS, HEAD_DIM), BF16),
            pltpu.VMEM((SEQ, 2, TROWS, HEAD_DIM), BF16),
            pltpu.VMEM((SEQ, ROWS, HEAD_DIM), BF16),
            pltpu.VMEM((OWNERS, ROWS, HEAD_DIM), BF16),
            pltpu.VMEM((1, HEAD_DIM), F32),
            pltpu.VMEM((2, HEADS, ROWS, HEAD_DIM), BF16),
            pltpu.VMEM((SEQ, 1, HEAD_DIM), F32),
            pltpu.SemaphoreType.DMA((9,)),
            pltpu.SemaphoreType.DMA((7,)),
            pltpu.SemaphoreType.DMA((7,)),
        ],
        compiler_params=pltpu.CompilerParams(collective_id=0, has_side_effects=True),
        name="joint_attention_step",
    )(
        text_len,
        step_index.reshape(1, 1),
        q_image,
        k_image,
        v_image,
        k_text,
        v_text,
        shift.reshape(1, HEADS, 1, HEAD_DIM),
        scale.reshape(1, HEADS, 1, HEAD_DIM),
        w_latent.T,
        latents,
    )
    latents_half, guided_half, norm, peaks = pl.pallas_call(
        hand_over,
        out_shape=shapes,
        in_specs=[anywhere] * 4,
        out_specs=[anywhere] * 4,
        scratch_shapes=[pltpu.SemaphoreType.DMA((4,))],
        name="hand_over",
    )(*results)
    return (latents_half, guided_half, norm.reshape(1), peaks.reshape(1, 1, HEADS))


def solution(mesh):
    placed = (
        P("cfg", ("req", "seq"), None),
        P("cfg", ("req", "seq"), None),
        P("cfg", ("req", "seq"), None),
        P("cfg", ("req", "seq"), None),
        P("cfg", ("req", "seq"), None),
        P("cfg", "req"),
        P("cfg", "req", None),
        P("cfg", "req", None),
        P(),
        P(("req", "seq"), None),
        P(),
    )
    return jax.shard_map(
        per_device,
        mesh=mesh,
        in_specs=placed,
        out_specs=(
            P(("req", "seq"), "cfg"),
            P(("req", "seq"), "cfg"),
            P("req"),
            P("cfg", "req", None),
        ),
        check_vma=False,
    )
```

time: 900 us -> 51.3 us (0.06)
  the two profiles are of different devices: /device:TPU:8 before, /device:TPU:1 now
where the time goes in v1:
time: 51.3 us; the launch traced here: 51.1 us
  Pallas kernels  49.2 us (96%)
  between operations  1.93 us (4%)
    pallas_call x1, Pallas kernels, per_device(): pl.pallas_call(kernel, out_shape=shapes, in_specs=[vmem] * 2 + [anywhere]...  47.2 us
    pallas_call x1, Pallas kernels, per_device(): pl.pallas_call(hand_over, out_shape=shapes, in_specs=[anywhere] * 4, out_...  2.01 us

profile of v1, /device:TPU:1, one launch (start us, length us, event | category | flops | bytes accessed | tf_op | source)
XLA Modules:
  0.0 51.1 jit_solution(15444733055852446445)
XLA Ops:
  1.9 47.2 %joint_attention_step.1 = (f32[8,32]{1,0:T(8,128)}, f32[8,32]{1,0:T(8,128)}, f32[1,1]{1,0:T(1,128)}, f32[1,16]{1,0:T(1,128)}) custom-call(s32[1,1]{1,0:T(1,128)S(6)} %copy.15.len_ref, s32[1,1]{1,0:T(1,128)} %bitcast.6.step_ref, bf16[1,8,2048]{2,1,0:T(8,128)(2,1)} %q_hbm.1, bf16[1,8,2048]{2,1,0:T(8,128)(2,1)} %k_hbm.1, bf16[1,8,2048]{2,1,0:T(8,128)(2,1)} %v_hbm.1, ...), custom_call_target="tpu_custom_call" | custom-call | tf_op jit(solution)/shard_map/joint_attention_step/pallas_call | solution.py:348
  49.1 2.0 %hand_over.1 = (f32[8,32]{1,0:T(8,128)}, f32[8,32]{1,0:T(8,128)}, f32[1,1]{1,0:T(1,128)}, f32[1,16]{1,0:T(1,128)}) custom-call(f32[8,32]{1,0:T(8,128)} %get-tuple-element.12.refs_0_, f32[8,32]{1,0:T(8,128)} %get-tuple-element.13.refs_1_, f32[1,1]{1,0:T(1,128)} %get-tuple-element.14.refs_2_, f32[1,16]{1,0:T(1,128)} %get-tuple-element.15.refs_3_), custom_call_target="tpu_custom_call" | custom-call | tf_op jit(solution)/shard_map/hand_over/pallas_call | solution.py:393

commit v2 on v1

v2 whole, which is shorter than its diff:
```python
import math

import jax
import jax.numpy as jnp
from jax import lax
from jax.experimental import pallas as pl
from jax.experimental.pallas import tpu as pltpu
from jax.sharding import PartitionSpec as P

HEADS = 16
HEAD_DIM = 128
FEAT = HEADS * HEAD_DIM
CHAN = 64
STEPS = 28
GUIDANCE = 3.5
SIGMA_SHIFT = 3.0

NZ, NX, NY = 8, 4, 4
SEQ = NZ * NX * NY
ROWS = 8
TROWS = 4
UZ = HEADS // NX
BLOCKS = 2
QY = NY // BLOCKS
OWNERS = NZ * NX * QY
CHUNK = 16
UNITS = HEADS * BLOCKS
FAR_4 = (2, 1, 3, 0)

MESH = pl.DeviceIdType.MESH
BF16 = jnp.bfloat16
F32 = jnp.float32


def remote(src, dst, send_sem, recv_sem, device):
    return pltpu.make_async_remote_copy(
        src_ref=src,
        dst_ref=dst,
        send_sem=send_sem,
        recv_sem=recv_sem,
        device_id=device,
        device_id_type=MESH,
    )


def wait_bytes(ref, sem):
    pltpu.make_async_copy(ref, ref, sem).wait()


def nt_dot(a, b):
    return lax.dot_general(a, b, (((1,), (1,)), ((), ())), preferred_element_type=F32)


def sigma_at(position):
    level = 1.0 - position / STEPS
    return SIGMA_SHIFT * level / (1.0 + (SIGMA_SHIFT - 1.0) * level)


def far_first(i):
    return NZ // 2 + ((i + 1) // 2) * (1 - 2 * lax.rem(i, 2))


def unit_y(z, x, block, cfg):
    return block if QY == 1 else block * QY + lax.rem(z + x + cfg, QY)


def over_z(body):
    def step(i, carry):
        body(far_first(i), False)
        return carry

    lax.fori_loop(0, NZ - 1, step, 0)
    body(0, True)


def kernel(
    len_ref,
    step_ref,
    q_hbm,
    k_hbm,
    v_hbm,
    kt_hbm,
    vt_hbm,
    shift_hbm,
    scale_hbm,
    w_hbm,
    lat_hbm,
    out_ref,
    w_own,
    lat_own,
    mod,
    q_all,
    k_all,
    kt_all,
    v_all,
    vt_all,
    att,
    peak_row,
    heads_in,
    sums,
    local_sem,
    send_sem,
    recv_sem,
):
    cfg = lax.axis_index("cfg")
    me = lax.axis_index("seq")
    other = 1 - cfg
    z = me // (NX * NY)
    x = lax.rem(me // NY, NX)
    y = lax.rem(me, NY)
    block = y // QY
    attends = (z < UZ) & (y == unit_y(z, x, block, cfg))
    idle = jnp.logical_not(attends)
    my_head = z * NX + x
    my_slot = (z * NX + x) * QY + lax.rem(y, QY)
    xs = [lax.rem(x + d, NX) for d in FAR_4]
    ys = [lax.rem(y + d, NY) for d in FAR_4]
    plane = [xx * NY + yy for xx in xs for yy in ys]

    loads = [
        (shift_hbm.at[0], mod.at[cfg, 0]),
        (scale_hbm.at[0], mod.at[cfg, 1]),
        (w_hbm, w_own),
        (lat_hbm, lat_own),
    ]
    copies = [pltpu.make_async_copy(s, d, local_sem.at[i]) for i, (s, d) in enumerate(loads)]
    for copy in copies:
        copy.start()

    barrier = pltpu.get_barrier_semaphore()

    def greet(device):
        pl.semaphore_signal(barrier, inc=1, device_id=device, device_id_type=MESH)

    greet({"cfg": other, "seq": me})

    @pl.when(attends)
    def _():
        def signals(dz, here):
            base = lax.rem(z + dz, NZ) * (NX * NY)
            for offset in plane[:-1] if here else plane:
                greet({"cfg": cfg, "seq": base + offset})

        over_z(signals)

    @pl.when(attends)
    def _():
        pl.semaphore_wait(barrier, UNITS)

    @pl.when(idle)
    def _():
        pl.semaphore_wait(barrier, UNITS + 1)

    def to_units(pieces):
        def sends(zz, here):
            for dx, xx in zip(FAR_4, xs):
                head = zz * NX + xx
                for db in reversed(range(BLOCKS)):
                    unit = head * NY + unit_y(zz, xx, lax.rem(block + db, BLOCKS), cfg)

                    def away():
                        for i, src, dst in pieces(head, db == 0):
                            device = {"cfg": cfg, "seq": unit}
                            remote(src, dst, send_sem.at[i], recv_sem.at[i], device).start()

                    def local():
                        for i, src, dst in pieces(head, True):
                            pltpu.make_async_copy(src, dst, recv_sem.at[i]).start()

                    if here and dx == 0 and db == 0:
                        pl.when(unit != me)(away)
                        pl.when(unit == me)(local)
                    else:
                        away()

        def step(i, carry):
            sends(lax.rem(z + 1 + i, UZ), False)
            return carry

        lax.fori_loop(0, UZ - 1, step, 0)
        sends(lax.rem(z, UZ), True)

    def slice_of(ref, head):
        return ref.at[0, :, pl.ds(pl.multiple_of(head * HEAD_DIM, HEAD_DIM), HEAD_DIM)]

    def keys(head, own_block):
        parts = [
            (0, slice_of(k_hbm, head), k_all.at[me]),
            (1, slice_of(kt_hbm, head), kt_all.at[me]),
        ]
        if own_block:
            parts.append((2, slice_of(q_hbm, head), q_all.at[my_slot]))
        return parts

    def values(head, own_block):
        return [
            (3, slice_of(v_hbm, head), v_all.at[me]),
            (7, slice_of(vt_hbm, head), vt_all.at[me]),
        ]

    to_units(keys)
    to_units(values)

    for copy in copies:
        copy.wait()
    mod_copy = remote(
        mod.at[cfg], mod.at[cfg], send_sem.at[4], recv_sem.at[4], {"cfg": other, "seq": me}
    )
    mod_copy.start()
    lane = lax.broadcasted_iota(jnp.int32, (1, HEAD_DIM), 1)
    peak_row[...] = jnp.full((1, HEAD_DIM), -jnp.inf)

    @pl.when(attends)
    def _():
        wait_bytes(k_all, recv_sem.at[0])
        wait_bytes(kt_all, recv_sem.at[1])
        wait_bytes(q_all, recv_sem.at[2])
        inv_root = 1.0 / math.sqrt(HEAD_DIM)
        rate = inv_root * math.log2(math.e)
        keys_image = k_all[...].reshape(SEQ * ROWS, HEAD_DIM)
        keys_text = kt_all[...].reshape(SEQ * TROWS, HEAD_DIM)
        position = lax.broadcasted_iota(jnp.int32, (1, SEQ * TROWS), 1)
        usable = position < len_ref[...]
        weights = []
        top = None
        for start in range(0, OWNERS, CHUNK):
            q = q_all[start : start + CHUNK].reshape(CHUNK * ROWS, HEAD_DIM)
            image = nt_dot(q, keys_image)
            text = jnp.where(usable, nt_dot(q, keys_text), -jnp.inf)
            peak = jnp.maximum(
                jnp.max(image, axis=1, keepdims=True), jnp.max(text, axis=1, keepdims=True)
            )
            image = jnp.exp2((image - peak) * rate).astype(BF16)
            text = jnp.exp2((text - peak) * rate).astype(BF16)
            weights.append((image, text))
            most = jnp.max(peak, axis=0, keepdims=True)
            top = most if top is None else jnp.maximum(top, most)
        peak_row[...] = jnp.where(lane == my_head, top * inv_root, -jnp.inf)
        ones = jnp.ones((SEQ * ROWS, HEAD_DIM), BF16)
        wait_bytes(v_all, recv_sem.at[3])
        wait_bytes(vt_all, recv_sem.at[7])
        v_image = jnp.concatenate([v_all[...].reshape(SEQ * ROWS, HEAD_DIM), ones], axis=1)
        v_text = jnp.concatenate(
            [vt_all[...].reshape(SEQ * TROWS, HEAD_DIM), ones[: SEQ * TROWS]], axis=1
        )
        for i, (image, text) in enumerate(weights):
            summed = jnp.dot(image, v_image, preferred_element_type=F32) + jnp.dot(
                text, v_text, preferred_element_type=F32
            )
            result = (summed[:, :HEAD_DIM] / summed[:, HEAD_DIM:]).astype(BF16)
            att[i * CHUNK : (i + 1) * CHUNK] = result.reshape(CHUNK, ROWS, HEAD_DIM)

        def give(dz, here):
            for dx, xx in zip(FAR_4, xs):
                for dy in reversed(range(QY)):
                    at_y = lax.rem(y + dy, QY)
                    base = lax.rem(z + dz, NZ) * NX + xx
                    slot = base * QY + at_y
                    owner = base * NY + (block * QY + at_y)
                    dst = heads_in.at[cfg, my_head]
                    for copy_index in (other, cfg):
                        if here and dx == 0 and dy == 0 and copy_index is cfg:
                            pltpu.make_async_copy(att.at[slot], dst, recv_sem.at[5]).start()
                        else:
                            device = {"cfg": copy_index, "seq": owner}
                            remote(
                                att.at[slot], dst, send_sem.at[5], recv_sem.at[5], device
                            ).start()

        over_z(give)

    mod_copy.wait_recv()
    wait_bytes(heads_in, recv_sem.at[5])
    parts = heads_in[...].astype(F32)
    average = jnp.sum(jnp.sum(parts, axis=1, keepdims=True), axis=3, keepdims=True) / FEAT
    parts = parts - average
    squares = jnp.sum(parts * parts, axis=1, keepdims=True)
    variance = jnp.sum(squares, axis=3, keepdims=True) / FEAT
    factor = lax.rsqrt(variance + 1e-06)
    normed = (parts * factor * (1.0 + mod[:, 1]) + mod[:, 0]).astype(BF16)
    normed = jnp.concatenate([normed[:, h] for h in range(HEADS)], axis=2)
    velocity = nt_dot(normed.reshape(2 * ROWS, FEAT), w_own[...])
    uncond = velocity[ROWS:]
    guided = uncond + GUIDANCE * (velocity[:ROWS] - uncond)
    position = jnp.broadcast_to(step_ref[...].astype(F32), (1, CHAN))
    delta = sigma_at(position + 1.0) - sigma_at(position)
    latents = lat_own[...] + delta * guided
    square = jnp.sum(
        jnp.sum(latents * latents, axis=1, keepdims=True), axis=0, keepdims=True
    )
    sums[me] = jnp.where(lane == HEADS, square, peak_row[...])

    def share(dz, here):
        base = lax.rem(z + dz, NZ) * (NX * NY)
        for offset in plane[:-1] if here else plane:
            remote(
                sums.at[me],
                sums.at[me],
                send_sem.at[6],
                recv_sem.at[6],
                {"cfg": cfg, "seq": base + offset},
            ).start()

    over_z(share)

    half = CHAN // 2
    out_ref[0, :, :half] = jnp.where(cfg == 0, latents[:, :half], latents[:, half:])
    out_ref[1, :, :half] = jnp.where(cfg == 0, guided[:, :half], guided[:, half:])

    mod_copy.wait_send()

    @pl.when(attends)
    def _():
        wait_bytes(k_all.at[: UNITS - 1], send_sem.at[0])
        wait_bytes(kt_all.at[: UNITS - 1], send_sem.at[1])
        wait_bytes(vt_all.at[: UNITS - 1], send_sem.at[7])
        wait_bytes(q_all.at[: HEADS - 1], send_sem.at[2])
        wait_bytes(v_all.at[: UNITS - 1], send_sem.at[3])
        wait_bytes(k_all.at[: 2 * OWNERS - 1], send_sem.at[5])

    @pl.when(idle)
    def _():
        wait_bytes(k_all.at[:UNITS], send_sem.at[0])
        wait_bytes(kt_all.at[:UNITS], send_sem.at[1])
        wait_bytes(vt_all.at[:UNITS], send_sem.at[7])
        wait_bytes(q_all.at[:HEADS], send_sem.at[2])
        wait_bytes(v_all.at[:UNITS], send_sem.at[3])

    wait_bytes(sums.at[: SEQ - 1], recv_sem.at[6])
    wait_bytes(sums.at[: SEQ - 1], send_sem.at[6])
    rows = sums[...]
    norm = jnp.sqrt(jnp.sum(rows, axis=0) / (SEQ * ROWS * CHAN))
    out_ref[2, 0:1, :] = jnp.where(lane == HEADS, norm, jnp.max(rows, axis=0))


def per_device(
    q_image, k_image, v_image, k_text, v_text, text_len, shift, scale, w_latent, latents, step_index
):
    anywhere = pl.BlockSpec(memory_space=pltpu.HBM)
    vmem = pl.BlockSpec(memory_space=pltpu.VMEM)
    half = CHAN // 2
    packed = pl.pallas_call(
        kernel,
        out_shape=pltpu.VMEM((3, ROWS, HEAD_DIM), F32),
        in_specs=[vmem] * 2 + [anywhere] * 9,
        out_specs=vmem,
        scratch_shapes=[
            pltpu.VMEM((CHAN, FEAT), BF16),
            pltpu.VMEM((ROWS, CHAN), F32),
            pltpu.VMEM((2, 2, HEADS, 1, HEAD_DIM), F32),
            pltpu.VMEM((OWNERS, ROWS, HEAD_DIM), BF16),
            pltpu.VMEM((SEQ, ROWS, HEAD_DIM), BF16),
            pltpu.VMEM((SEQ, TROWS, HEAD_DIM), BF16),
            pltpu.VMEM((SEQ, ROWS, HEAD_DIM), BF16),
            pltpu.VMEM((SEQ, TROWS, HEAD_DIM), BF16),
            pltpu.VMEM((OWNERS, ROWS, HEAD_DIM), BF16),
            pltpu.VMEM((1, HEAD_DIM), F32),
            pltpu.VMEM((2, HEADS, ROWS, HEAD_DIM), BF16),
            pltpu.VMEM((SEQ, 1, HEAD_DIM), F32),
            pltpu.SemaphoreType.DMA((4,)),
            pltpu.SemaphoreType.DMA((8,)),
            pltpu.SemaphoreType.DMA((8,)),
        ],
        compiler_params=pltpu.CompilerParams(collective_id=0, has_side_effects=True),
        name="joint_attention_step",
    )(
        text_len,
        step_index.reshape(1, 1),
        q_image,
        k_image,
        v_image,
        k_text,
        v_text,
        shift.reshape(1, HEADS, 1, HEAD_DIM),
        scale.reshape(1, HEADS, 1, HEAD_DIM),
        w_latent.T,
        latents,
    )
    return (
        packed[0, :, :half],
        packed[1, :, :half],
        packed[2, 0, HEADS : HEADS + 1],
        packed[2, 0:1, :HEADS].reshape(1, 1, HEADS),
    )


def solution(mesh):
    placed = (
        P("cfg", ("req", "seq"), None),
        P("cfg", ("req", "seq"), None),
        P("cfg", ("req", "seq"), None),
        P("cfg", ("req", "seq"), None),
        P("cfg", ("req", "seq"), None),
        P("cfg", "req"),
        P("cfg", "req", None),
        P("cfg", "req", None),
        P(),
        P(("req", "seq"), None),
        P(),
    )
    return jax.shard_map(
        per_device,
        mesh=mesh,
        in_specs=placed,
        out_specs=(
            P(("req", "seq"), "cfg"),
            P(("req", "seq"), "cfg"),
            P("req"),
            P("cfg", "req", None),
        ),
        check_vma=False,
    )
```

time: 51.3 us -> 48.1 us (0.938)
  Pallas kernels: 49.2 us -> 44.4 us
  local copies, waits for them, and re-layouts: 0 us -> 1.69 us
    pallas_call x2 -> x1, Pallas kernels: 49.2 us -> 44.4 us  [per_device(): pl.pallas_call(kernel, out_shape=pltpu.VMEM((3, ROWS, HEAD_DIM), F32), in...]
    slice x0 -> x2, local copies, waits for them, and re-layouts: none -> 1.09 us  [the longest x1 0.58 us: per_device(): packed[2, 0, HEADS:HEADS + 1]]
    squeeze x0 -> x1, local copies, waits for them, and re-layouts: none -> 0.6 us  [per_device(): packed[1, :, :half]]
where the time goes in v2:
time: 48.1 us; the launch traced here: 48 us
  Pallas kernels  44.4 us (92%)
  between operations  1.94 us (4%)
  local copies, waits for them, and re-layouts  1.69 us (4%)
    pallas_call x1, Pallas kernels, per_device(): pl.pallas_call(kernel, out_shape=pltpu.VMEM((3, ROWS, HEAD_DIM), F32), in...  44.4 us

profile of v2, /device:TPU:1, one launch (start us, length us, event | category | flops | bytes accessed | tf_op | source)
XLA Modules:
  0.0 48.0 jit_solution(13963002128784606379)
XLA Ops:
  1.9 44.4 %joint_attention_step.1 = f32[3,8,128]{2,1,0:T(8,128)S(1)} custom-call(s32[1,1]{1,0:T(1,128)S(6)} %copy.15.len_ref, s32[1,1]{1,0:T(1,128)} %bitcast.9.step_ref, bf16[1,8,2048]{2,1,0:T(8,128)(2,1)} %q_hbm.1, bf16[1,8,2048]{2,1,0:T(8,128)(2,1)} %k_hbm.1, bf16[1,8,2048]{2,1,0:T(8,128)(2,1)} %v_hbm.1, bf16[1,4,2048]{2,1,0:T(4,128)(2,1)} %kt_hbm.1, ...), custom_call_target="tpu_custom_call" | custom-call | tf_op jit(solution)/shard_map/joint_attention_step/pallas_call | solution.py:342
  46.3 0.6 %slice_bitcast_fusion = (f32[8,32]{1,0:T(8,128)}, f32[8,32]{1,0:T(8,128)}) fusion(f32[3,8,128]{2,1,0:T(8,128)S(1)} %joint_attention_step.1), kind=kLoop, calls=%fused_computation | loop fusion | bytes 4096 | tf_op jit(solution)/shard_map/squeeze | solution.py:381
  46.9 0.6 %slice.14 = f32[1,1,1]{2,1,0:T(1,128)} slice(f32[3,8,128]{2,1,0:T(8,128)S(1)} %joint_attention_step.1), slice={[2:3], [0:1], [16:17]} | slice | bytes 8 | tf_op jit(solution)/shard_map/slice | solution.py:382
  47.5 0.5 %slice.15 = f32[1,1,16]{2,1,0:T(1,128)} slice(f32[3,8,128]{2,1,0:T(8,128)S(1)} %joint_attention_step.1), slice={[2:3], [0:1], [0:16]} | slice | bytes 128 | tf_op jit(solution)/shard_map/slice | solution.py:383

commit v3 on v2

--- a/solution.py
+++ b/solution.py
@@ -23,6 +23,11 @@
 BLOCKS = 2
 QY = NY // BLOCKS
 OWNERS = NZ * NX * QY
+LZ = 1
+LFROM = 1
+OPL = NZ // (2 * LZ)
+FINAL = 2 * LZ * NX * NY
+FINAL_BLOCK = FINAL // BLOCKS
 CHUNK = 16
 UNITS = HEADS * BLOCKS
 FAR_4 = (2, 1, 3, 0)
@@ -87,7 +92,7 @@
     lat_hbm,
     out_ref,
     w_own,
-    lat_own,
+    lat_in,
     mod,
     q_all,
     k_all,
@@ -97,6 +102,9 @@
     att,
     peak_row,
     heads_in,
+    peaks_in,
+    result,
+    result_in,
     sums,
     local_sem,
     send_sem,
@@ -112,7 +120,15 @@
     attends = (z < UZ) & (y == unit_y(z, x, block, cfg))
     idle = jnp.logical_not(attends)
     my_head = z * NX + x
-    my_slot = (z * NX + x) * QY + lax.rem(y, QY)
+    group = z // OPL
+    my_slot = ((group * NX + x) * QY + lax.rem(y, QY)) * OPL + lax.rem(z, OPL)
+    finishes = (z >= LFROM) & (z < LFROM + LZ)
+    passes = (z < LFROM) | (z >= LFROM + LZ)
+    my_group = cfg * LZ + z - LFROM
+    my_row = (my_group * NX + x) * NY + y
+    gives = cfg == group // LZ
+    keeps = gives & (LFROM + lax.rem(group, LZ) == z)
+    sends_lat = gives & (LFROM + lax.rem(group, LZ) != z)
     xs = [lax.rem(x + d, NX) for d in FAR_4]
     ys = [lax.rem(y + d, NY) for d in FAR_4]
     plane = [xx * NY + yy for xx in xs for yy in ys]
@@ -121,11 +137,8 @@
         (shift_hbm.at[0], mod.at[cfg, 0]),
         (scale_hbm.at[0], mod.at[cfg, 1]),
         (w_hbm, w_own),
-        (lat_hbm, lat_own),
     ]
     copies = [pltpu.make_async_copy(s, d, local_sem.at[i]) for i, (s, d) in enumerate(loads)]
-    for copy in copies:
-        copy.start()
 
     barrier = pltpu.get_barrier_semaphore()
 
@@ -143,13 +156,21 @@
 
         over_z(signals)
 
-    @pl.when(attends)
-    def _():
-        pl.semaphore_wait(barrier, UNITS)
-
-    @pl.when(idle)
-    def _():
-        pl.semaphore_wait(barrier, UNITS + 1)
+    @pl.when(finishes)
+    def _():
+        for j in range(OPL):
+            owner_z = my_group * OPL + j
+
+            @pl.when(owner_z != z)
+            def _():
+                greet({"cfg": cfg, "seq": (owner_z * NX + x) * NY + y})
+
+        for copy in copies:
+            copy.start()
+
+    pl.semaphore_wait(
+        barrier, UNITS + 1 - jnp.where(attends, 1, 0) + jnp.where(sends_lat, 1, 0)
+    )
 
     def to_units(pieces):
         def sends(zz, here):
@@ -201,14 +222,30 @@
     to_units(keys)
     to_units(values)
 
-    for copy in copies:
-        copy.wait()
     mod_copy = remote(
         mod.at[cfg], mod.at[cfg], send_sem.at[4], recv_sem.at[4], {"cfg": other, "seq": me}
     )
-    mod_copy.start()
+    taker = ((LFROM + lax.rem(group, LZ)) * NX + x) * NY + y
+    lat_slot = lat_in.at[lax.rem(z, OPL)]
+    lat_copy = remote(
+        lat_hbm, lat_slot, send_sem.at[8], recv_sem.at[8], {"cfg": cfg, "seq": taker}
+    )
+
+    @pl.when(sends_lat)
+    def _():
+        lat_copy.start()
+
+    @pl.when(keeps)
+    def _():
+        pltpu.make_async_copy(lat_hbm, lat_slot, recv_sem.at[8]).start()
+
+    @pl.when(finishes)
+    def _():
+        for copy in copies:
+            copy.wait()
+        mod_copy.start()
+
     lane = lax.broadcasted_iota(jnp.int32, (1, HEAD_DIM), 1)
-    peak_row[...] = jnp.full((1, HEAD_DIM), -jnp.inf)
 
     @pl.when(attends)
     def _():
@@ -235,7 +272,7 @@
             weights.append((image, text))
             most = jnp.max(peak, axis=0, keepdims=True)
             top = most if top is None else jnp.maximum(top, most)
-        peak_row[...] = jnp.where(lane == my_head, top * inv_root, -jnp.inf)
+        peak_row[...] = jnp.where(lane == cfg * HEADS + my_head, top * inv_root, -jnp.inf)
         ones = jnp.ones((SEQ * ROWS, HEAD_DIM), BF16)
         wait_bytes(v_all, recv_sem.at[3])
         wait_bytes(vt_all, recv_sem.at[7])
@@ -250,87 +287,166 @@
             result = (summed[:, :HEAD_DIM] / summed[:, HEAD_DIM:]).astype(BF16)
             att[i * CHUNK : (i + 1) * CHUNK] = result.reshape(CHUNK, ROWS, HEAD_DIM)
 
-        def give(dz, here):
-            for dx, xx in zip(FAR_4, xs):
-                for dy in reversed(range(QY)):
-                    at_y = lax.rem(y + dy, QY)
-                    base = lax.rem(z + dz, NZ) * NX + xx
-                    slot = base * QY + at_y
-                    owner = base * NY + (block * QY + at_y)
-                    dst = heads_in.at[cfg, my_head]
+        for dx, xx in zip(FAR_4, xs):
+            for dy in reversed(range(QY)):
+                at_y = lax.rem(y + dy, QY)
+                for plane_z in reversed(range(LZ)):
+                    target = ((LFROM + plane_z) * NX + xx) * NY + (block * QY + at_y)
                     for copy_index in (other, cfg):
-                        if here and dx == 0 and dy == 0 and copy_index is cfg:
-                            pltpu.make_async_copy(att.at[slot], dst, recv_sem.at[5]).start()
+                        k = copy_index * LZ + plane_z
+                        first = ((k * NX + xx) * QY + at_y) * OPL
+                        moves = [
+                            (5, att.at[pl.ds(first, OPL)], heads_in.at[cfg, my_head]),
+                            (9, peak_row, peaks_in.at[cfg, my_head]),
+                        ]
+
+                        def away():
+                            device = {"cfg": copy_index, "seq": target}
+                            for i, src, dst in moves:
+                                remote(src, dst, send_sem.at[i], recv_sem.at[i], device).start()
+
+                        def local():
+                            for i, src, dst in moves:
+                                pltpu.make_async_copy(src, dst, recv_sem.at[i]).start()
+
+                        if dx == 0 and dy == 0 and copy_index is cfg:
+                            pl.when(LFROM + plane_z != z)(away)
+                            pl.when(LFROM + plane_z == z)(local)
                         else:
-                            device = {"cfg": copy_index, "seq": owner}
-                            remote(
-                                att.at[slot], dst, send_sem.at[5], recv_sem.at[5], device
-                            ).start()
-
-        over_z(give)
-
-    mod_copy.wait_recv()
-    wait_bytes(heads_in, recv_sem.at[5])
-    parts = heads_in[...].astype(F32)
-    average = jnp.sum(jnp.sum(parts, axis=1, keepdims=True), axis=3, keepdims=True) / FEAT
-    parts = parts - average
-    squares = jnp.sum(parts * parts, axis=1, keepdims=True)
-    variance = jnp.sum(squares, axis=3, keepdims=True) / FEAT
-    factor = lax.rsqrt(variance + 1e-06)
-    normed = (parts * factor * (1.0 + mod[:, 1]) + mod[:, 0]).astype(BF16)
-    normed = jnp.concatenate([normed[:, h] for h in range(HEADS)], axis=2)
-    velocity = nt_dot(normed.reshape(2 * ROWS, FEAT), w_own[...])
-    uncond = velocity[ROWS:]
-    guided = uncond + GUIDANCE * (velocity[:ROWS] - uncond)
-    position = jnp.broadcast_to(step_ref[...].astype(F32), (1, CHAN))
-    delta = sigma_at(position + 1.0) - sigma_at(position)
-    latents = lat_own[...] + delta * guided
-    square = jnp.sum(
-        jnp.sum(latents * latents, axis=1, keepdims=True), axis=0, keepdims=True
-    )
-    sums[me] = jnp.where(lane == HEADS, square, peak_row[...])
-
-    def share(dz, here):
-        base = lax.rem(z + dz, NZ) * (NX * NY)
-        for offset in plane[:-1] if here else plane:
-            remote(
-                sums.at[me],
-                sums.at[me],
-                send_sem.at[6],
-                recv_sem.at[6],
-                {"cfg": cfg, "seq": base + offset},
-            ).start()
-
-    over_z(share)
-
+                            away()
+
+    @pl.when(finishes)
+    def _():
+        mod_copy.wait_recv()
+        wait_bytes(lat_in, recv_sem.at[8])
+        wait_bytes(heads_in, recv_sem.at[5])
+        wait_bytes(peaks_in, recv_sem.at[9])
+        parts = heads_in[...].astype(F32)
+        average = jnp.sum(jnp.sum(parts, axis=1, keepdims=True), axis=4, keepdims=True) / FEAT
+        parts = parts - average
+        squares = jnp.sum(parts * parts, axis=1, keepdims=True)
+        variance = jnp.sum(squares, axis=4, keepdims=True) / FEAT
+        factor = lax.rsqrt(variance + 1e-06)
+        normed = parts * factor * (1.0 + mod[:, 1][:, :, None]) + mod[:, 0][:, :, None]
+        normed = normed.reshape(2, HEADS, OPL * ROWS, HEAD_DIM).astype(BF16)
+        normed = jnp.concatenate([normed[:, h] for h in range(HEADS)], axis=2)
+        velocity = nt_dot(normed.reshape(2 * OPL * ROWS, FEAT), w_own[...])
+        uncond = velocity[OPL * ROWS :]
+        guided = uncond + GUIDANCE * (velocity[: OPL * ROWS] - uncond)
+        position = jnp.broadcast_to(step_ref[...].astype(F32), (1, CHAN))
+        delta = sigma_at(position + 1.0) - sigma_at(position)
+        latents = lat_in[...].reshape(OPL * ROWS, CHAN) + delta * guided
+        square = jnp.sum(
+            jnp.sum(latents * latents, axis=1, keepdims=True), axis=0, keepdims=True
+        )
+        tops = jnp.max(peaks_in[...].reshape(2 * HEADS, 1, HEAD_DIM), axis=0)
+        sums[my_row] = jnp.where(lane == 2 * HEADS, square, tops)
+        done = jnp.concatenate([latents, guided], axis=1)
+        result[:OPL] = done.reshape(OPL, ROWS, HEAD_DIM)
+
+        def share(base, skip):
+            for offset in plane:
+                for copy_index in (cfg, other):
+                    if skip and offset is plane[-1] and copy_index is cfg:
+                        continue
+                    remote(
+                        sums.at[my_row],
+                        sums.at[my_row],
+                        send_sem.at[6],
+                        recv_sem.at[6],
+                        {"cfg": copy_index, "seq": base + offset},
+                    ).start()
+
+        share(lax.rem(z + NZ - 1, NZ) * (NX * NY), False)
+        share(z * (NX * NY), True)
+        for j in range(OPL):
+            owner_z = my_group * OPL + j
+            for copy_index in (cfg, other):
+
+                def away():
+                    device = {"cfg": copy_index, "seq": (owner_z * NX + x) * NY + y}
+                    remote(
+                        result.at[j], result_in, send_sem.at[10], recv_sem.at[10], device
+                    ).start()
+
+                def local():
+                    pltpu.make_async_copy(result.at[j], result_in, recv_sem.at[10]).start()
+
+                if copy_index is cfg:
+                    pl.when(owner_z != z)(away)
+                    pl.when(owner_z == z)(local)
+                else:
+                    away()
+
+        def step(i, carry):
+            share(lax.rem(z + 1 + i, NZ) * (NX * NY), False)
+            return carry
+
+        lax.fori_loop(0, NZ - 2, step, 0)
+
+    wait_bytes(result_in, recv_sem.at[10])
+    latents = result_in[:, :CHAN]
+    guided = result_in[:, CHAN:]
     half = CHAN // 2
     out_ref[0, :, :half] = jnp.where(cfg == 0, latents[:, :half], latents[:, half:])
     out_ref[1, :, :half] = jnp.where(cfg == 0, guided[:, :half], guided[:, half:])
 
-    mod_copy.wait_send()
+    @pl.when(sends_lat)
+    def _():
+        lat_copy.wait_send()
 
     @pl.when(attends)
     def _():
         wait_bytes(k_all.at[: UNITS - 1], send_sem.at[0])
         wait_bytes(kt_all.at[: UNITS - 1], send_sem.at[1])
-        wait_bytes(vt_all.at[: UNITS - 1], send_sem.at[7])
         wait_bytes(q_all.at[: HEADS - 1], send_sem.at[2])
         wait_bytes(v_all.at[: UNITS - 1], send_sem.at[3])
-        wait_bytes(k_all.at[: 2 * OWNERS - 1], send_sem.at[5])
+        wait_bytes(vt_all.at[: UNITS - 1], send_sem.at[7])
 
     @pl.when(idle)
     def _():
         wait_bytes(k_all.at[:UNITS], send_sem.at[0])
         wait_bytes(kt_all.at[:UNITS], send_sem.at[1])
-        wait_bytes(vt_all.at[:UNITS], send_sem.at[7])
         wait_bytes(q_all.at[:HEADS], send_sem.at[2])
         wait_bytes(v_all.at[:UNITS], send_sem.at[3])
-
-    wait_bytes(sums.at[: SEQ - 1], recv_sem.at[6])
-    wait_bytes(sums.at[: SEQ - 1], send_sem.at[6])
-    rows = sums[...]
+        wait_bytes(vt_all.at[:UNITS], send_sem.at[7])
+
+    @pl.when(attends & finishes)
+    def _():
+        wait_bytes(att.at[: OWNERS - OPL], send_sem.at[5])
+        wait_bytes(sums.at[: FINAL_BLOCK - 1], send_sem.at[9])
+
+    @pl.when(attends & passes)
+    def _():
+        wait_bytes(att, send_sem.at[5])
+        wait_bytes(sums.at[:FINAL_BLOCK], send_sem.at[9])
+
+    @pl.when(finishes)
+    def _():
+        mod_copy.wait_send()
+        wait_bytes(sums.at[: FINAL - 1], recv_sem.at[6])
+
+    @pl.when(passes)
+    def _():
+        wait_bytes(sums.at[:FINAL], recv_sem.at[6])
+
+    rows = sums[:FINAL]
     norm = jnp.sqrt(jnp.sum(rows, axis=0) / (SEQ * ROWS * CHAN))
-    out_ref[2, 0:1, :] = jnp.where(lane == HEADS, norm, jnp.max(rows, axis=0))
+    tops = jnp.max(rows, axis=0)
+    out_ref[2, 0:1, :HEADS] = jnp.where(cfg == 0, tops[:, :HEADS], tops[:, HEADS : 2 * HEADS])
+    out_ref[2, 1:2, :] = norm
+
+    @pl.when(finishes)
+    def _():
+        wait_bytes(sums.at[: 2 * SEQ - 1], send_sem.at[6])
+
+    @pl.when(finishes & keeps)
+    def _():
+        wait_bytes(result.at[: 2 * OPL - 1], send_sem.at[10])
+
+    @pl.when(finishes & jnp.logical_not(keeps))
+    def _():
+        wait_bytes(result, send_sem.at[10])
 
 
 def per_device(
@@ -346,7 +462,7 @@
         out_specs=vmem,
         scratch_shapes=[
             pltpu.VMEM((CHAN, FEAT), BF16),
-            pltpu.VMEM((ROWS, CHAN), F32),
+            pltpu.VMEM((OPL, ROWS, CHAN), F32),
             pltpu.VMEM((2, 2, HEADS, 1, HEAD_DIM), F32),
             pltpu.VMEM((OWNERS, ROWS, HEAD_DIM), BF16),
             pltpu.VMEM((SEQ, ROWS, HEAD_DIM), BF16),
@@ -355,11 +471,14 @@
             pltpu.VMEM((SEQ, TROWS, HEAD_DIM), BF16),
             pltpu.VMEM((OWNERS, ROWS, HEAD_DIM), BF16),
             pltpu.VMEM((1, HEAD_DIM), F32),
-            pltpu.VMEM((2, HEADS, ROWS, HEAD_DIM), BF16),
-            pltpu.VMEM((SEQ, 1, HEAD_DIM), F32),
-            pltpu.SemaphoreType.DMA((4,)),
-            pltpu.SemaphoreType.DMA((8,)),
-            pltpu.SemaphoreType.DMA((8,)),
+            pltpu.VMEM((2, HEADS, OPL, ROWS, HEAD_DIM), BF16),
+            pltpu.VMEM((2, HEADS, 1, HEAD_DIM), F32),
+            pltpu.VMEM((2 * OPL, ROWS, HEAD_DIM), F32),
+            pltpu.VMEM((ROWS, HEAD_DIM), F32),
+            pltpu.VMEM((2 * SEQ, 1, HEAD_DIM), F32),
+            pltpu.SemaphoreType.DMA((3,)),
+            pltpu.SemaphoreType.DMA((11,)),
+            pltpu.SemaphoreType.DMA((11,)),
         ],
         compiler_params=pltpu.CompilerParams(collective_id=0, has_side_effects=True),
         name="joint_attention_step",
@@ -379,7 +498,7 @@
     return (
         packed[0, :, :half],
         packed[1, :, :half],
-        packed[2, 0, HEADS : HEADS + 1],
+        packed[2, 1, 2 * HEADS : 2 * HEADS + 1],
         packed[2, 0:1, :HEADS].reshape(1, 1, HEADS),
     )
 

time: 48.1 us -> 45.8 us (0.952)
  Pallas kernels: 44.4 us -> 42.1 us
    pallas_call x1, Pallas kernels: 44.4 us -> 42.1 us  [per_device(): pl.pallas_call(kernel, out_shape=pltpu.VMEM((3, ROWS, HEAD_DIM), F32), in...]
where the time goes in v3:
time: 45.8 us; the launch traced here: 45.7 us
  Pallas kernels  42.1 us (92%)
  between operations  1.94 us (4%)
  local copies, waits for them, and re-layouts  1.69 us (4%)
    pallas_call x1, Pallas kernels, per_device(): pl.pallas_call(kernel, out_shape=pltpu.VMEM((3, ROWS, HEAD_DIM), F32), in...  42.1 us

profile of v3, /device:TPU:1, one launch (start us, length us, event | category | flops | bytes accessed | tf_op | source)
XLA Modules:
  0.0 45.7 jit_solution(5115546389526050198)
XLA Ops:
  1.9 42.1 %joint_attention_step.1 = f32[3,8,128]{2,1,0:T(8,128)S(1)} custom-call(s32[1,1]{1,0:T(1,128)S(6)} %copy.15.len_ref, s32[1,1]{1,0:T(1,128)} %bitcast.9.step_ref, bf16[1,8,2048]{2,1,0:T(8,128)(2,1)} %q_hbm.1, bf16[1,8,2048]{2,1,0:T(8,128)(2,1)} %k_hbm.1, bf16[1,8,2048]{2,1,0:T(8,128)(2,1)} %v_hbm.1, bf16[1,4,2048]{2,1,0:T(4,128)(2,1)} %kt_hbm.1, ...), custom_call_target="tpu_custom_call" | custom-call | tf_op jit(solution)/shard_map/joint_attention_step/pallas_call | solution.py:458
  44.0 0.6 %slice_bitcast_fusion = (f32[8,32]{1,0:T(8,128)}, f32[8,32]{1,0:T(8,128)}) fusion(f32[3,8,128]{2,1,0:T(8,128)S(1)} %joint_attention_step.1), kind=kLoop, calls=%fused_computation | loop fusion | bytes 4096 | tf_op jit(solution)/shard_map/squeeze | solution.py:500
  44.6 0.6 %slice.14 = f32[1,1,1]{2,1,0:T(1,128)} slice(f32[3,8,128]{2,1,0:T(8,128)S(1)} %joint_attention_step.1), slice={[2:3], [1:2], [32:33]} | slice | bytes 8 | tf_op jit(solution)/shard_map/slice | solution.py:501
  45.2 0.5 %slice.15 = f32[1,1,16]{2,1,0:T(1,128)} slice(f32[3,8,128]{2,1,0:T(8,128)S(1)} %joint_attention_step.1), slice={[2:3], [0:1], [0:16]} | slice | bytes 128 | tf_op jit(solution)/shard_map/slice | solution.py:502

commit v4 on v3

--- a/solution.py
+++ b/solution.py
@@ -91,6 +91,11 @@
     w_hbm,
     lat_hbm,
     out_ref,
+    q_own,
+    k_own,
+    v_own,
+    kt_own,
+    vt_own,
     w_own,
     lat_in,
     mod,
@@ -133,6 +138,18 @@
     ys = [lax.rem(y + d, NY) for d in FAR_4]
     plane = [xx * NY + yy for xx in xs for yy in ys]
 
+    sources = [
+        (k_hbm, k_own),
+        (kt_hbm, kt_own),
+        (q_hbm, q_own),
+        (v_hbm, v_own),
+        (vt_hbm, vt_own),
+    ]
+    staged = [
+        pltpu.make_async_copy(s.at[0], d, local_sem.at[3 + i]) for i, (s, d) in enumerate(sources)
+    ]
+    for copy in staged:
+        copy.start()
     loads = [
         (shift_hbm.at[0], mod.at[cfg, 0]),
         (scale_hbm.at[0], mod.at[cfg, 1]),
@@ -172,6 +189,9 @@
         barrier, UNITS + 1 - jnp.where(attends, 1, 0) + jnp.where(sends_lat, 1, 0)
     )
 
+    for copy in staged:
+        copy.wait()
+
     def to_units(pieces):
         def sends(zz, here):
             for dx, xx in zip(FAR_4, xs):
@@ -194,29 +214,31 @@
                     else:
                         away()
 
+        near = jnp.where(z < UZ, z + 1, z)
+
         def step(i, carry):
-            sends(lax.rem(z + 1 + i, UZ), False)
+            sends(lax.rem(near + i, UZ), False)
             return carry
 
         lax.fori_loop(0, UZ - 1, step, 0)
-        sends(lax.rem(z, UZ), True)
+        sends(lax.rem(near + UZ - 1, UZ), True)
 
     def slice_of(ref, head):
-        return ref.at[0, :, pl.ds(pl.multiple_of(head * HEAD_DIM, HEAD_DIM), HEAD_DIM)]
+        return ref.at[:, pl.ds(pl.multiple_of(head * HEAD_DIM, HEAD_DIM), HEAD_DIM)]
 
     def keys(head, own_block):
         parts = [
-            (0, slice_of(k_hbm, head), k_all.at[me]),
-            (1, slice_of(kt_hbm, head), kt_all.at[me]),
+            (0, slice_of(k_own, head), k_all.at[me]),
+            (1, slice_of(kt_own, head), kt_all.at[me]),
         ]
         if own_block:
-            parts.append((2, slice_of(q_hbm, head), q_all.at[my_slot]))
+            parts.append((2, slice_of(q_own, head), q_all.at[my_slot]))
         return parts
 
     def values(head, own_block):
         return [
-            (3, slice_of(v_hbm, head), v_all.at[me]),
-            (7, slice_of(vt_hbm, head), vt_all.at[me]),
+            (3, slice_of(v_own, head), v_all.at[me]),
+            (7, slice_of(vt_own, head), vt_all.at[me]),
         ]
 
     to_units(keys)
@@ -461,6 +483,11 @@
         in_specs=[vmem] * 2 + [anywhere] * 9,
         out_specs=vmem,
         scratch_shapes=[
+            pltpu.VMEM((ROWS, FEAT), BF16),
+            pltpu.VMEM((ROWS, FEAT), BF16),
+            pltpu.VMEM((ROWS, FEAT), BF16),
+            pltpu.VMEM((TROWS, FEAT), BF16),
+            pltpu.VMEM((TROWS, FEAT), BF16),
             pltpu.VMEM((CHAN, FEAT), BF16),
             pltpu.VMEM((OPL, ROWS, CHAN), F32),
             pltpu.VMEM((2, 2, HEADS, 1, HEAD_DIM), F32),
@@ -476,7 +503,7 @@
             pltpu.VMEM((2 * OPL, ROWS, HEAD_DIM), F32),
             pltpu.VMEM((ROWS, HEAD_DIM), F32),
             pltpu.VMEM((2 * SEQ, 1, HEAD_DIM), F32),
-            pltpu.SemaphoreType.DMA((3,)),
+            pltpu.SemaphoreType.DMA((8,)),
             pltpu.SemaphoreType.DMA((11,)),
             pltpu.SemaphoreType.DMA((11,)),
         ],

time: 45.8 us -> 45.8 us (level)
  no operation moved by 1% of the time
where the time goes in v4:
time: 45.8 us; the launch traced here: 45.6 us
  Pallas kernels  42 us (92%)
  between operations  1.94 us (4%)
  local copies, waits for them, and re-layouts  1.69 us (4%)
    pallas_call x1, Pallas kernels, per_device(): pl.pallas_call(kernel, out_shape=pltpu.VMEM((3, ROWS, HEAD_DIM), F32), in...  42 us

profile of v4, /device:TPU:1, one launch (start us, length us, event | category | flops | bytes accessed | tf_op | source)
XLA Modules:
  0.0 45.6 jit_solution(17597998570653704259)
XLA Ops:
  1.9 42.0 %joint_attention_step.1 = f32[3,8,128]{2,1,0:T(8,128)S(1)} custom-call(s32[1,1]{1,0:T(1,128)S(6)} %copy.15.len_ref, s32[1,1]{1,0:T(1,128)} %bitcast.9.step_ref, bf16[1,8,2048]{2,1,0:T(8,128)(2,1)} %q_hbm.1, bf16[1,8,2048]{2,1,0:T(8,128)(2,1)} %k_hbm.1, bf16[1,8,2048]{2,1,0:T(8,128)(2,1)} %v_hbm.1, bf16[1,4,2048]{2,1,0:T(4,128)(2,1)} %kt_hbm.1, ...), custom_call_target="tpu_custom_call" | custom-call | tf_op jit(solution)/shard_map/joint_attention_step/pallas_call | solution.py:480
  43.9 0.6 %slice_bitcast_fusion = (f32[8,32]{1,0:T(8,128)}, f32[8,32]{1,0:T(8,128)}) fusion(f32[3,8,128]{2,1,0:T(8,128)S(1)} %joint_attention_step.1), kind=kLoop, calls=%fused_computation | loop fusion | bytes 4096 | tf_op jit(solution)/shard_map/squeeze | solution.py:527
  44.5 0.6 %slice.14 = f32[1,1,1]{2,1,0:T(1,128)} slice(f32[3,8,128]{2,1,0:T(8,128)S(1)} %joint_attention_step.1), slice={[2:3], [1:2], [32:33]} | slice | bytes 8 | tf_op jit(solution)/shard_map/slice | solution.py:528
  45.1 0.5 %slice.15 = f32[1,1,16]{2,1,0:T(1,128)} slice(f32[3,8,128]{2,1,0:T(8,128)S(1)} %joint_attention_step.1), slice={[2:3], [0:1], [0:16]} | slice | bytes 128 | tf_op jit(solution)/shard_map/slice | solution.py:529

commit v5 on v4

--- a/solution.py
+++ b/solution.py
@@ -148,8 +148,6 @@
     staged = [
         pltpu.make_async_copy(s.at[0], d, local_sem.at[3 + i]) for i, (s, d) in enumerate(sources)
     ]
-    for copy in staged:
-        copy.start()
     loads = [
         (shift_hbm.at[0], mod.at[cfg, 0]),
         (scale_hbm.at[0], mod.at[cfg, 1]),
@@ -171,7 +169,12 @@
             for offset in plane[:-1] if here else plane:
                 greet({"cfg": cfg, "seq": base + offset})
 
-        over_z(signals)
+        for dz in (4, 3, 5, 2, 6, 1, 7):
+            signals(dz, False)
+        signals(0, True)
+
+    for copy in staged:
+        copy.start()
 
     @pl.when(finishes)
     def _():

time: 45.8 us -> 45.8 us (level)
  no operation moved by 1% of the time
where the time goes in v5:
time: 45.8 us; the launch traced here: 45.6 us
  Pallas kernels  42 us (92%)
  between operations  1.94 us (4%)
  local copies, waits for them, and re-layouts  1.69 us (4%)
    pallas_call x1, Pallas kernels, per_device(): pl.pallas_call(kernel, out_shape=pltpu.VMEM((3, ROWS, HEAD_DIM), F32), in...  42 us

profile of v5, /device:TPU:1, one launch (start us, length us, event | category | flops | bytes accessed | tf_op | source)
XLA Modules:
  0.0 45.6 jit_solution(2492963190810752016)
XLA Ops:
  1.9 42.0 %joint_attention_step.1 = f32[3,8,128]{2,1,0:T(8,128)S(1)} custom-call(s32[1,1]{1,0:T(1,128)S(6)} %copy.15.len_ref, s32[1,1]{1,0:T(1,128)} %bitcast.9.step_ref, bf16[1,8,2048]{2,1,0:T(8,128)(2,1)} %q_hbm.1, bf16[1,8,2048]{2,1,0:T(8,128)(2,1)} %k_hbm.1, bf16[1,8,2048]{2,1,0:T(8,128)(2,1)} %v_hbm.1, bf16[1,4,2048]{2,1,0:T(4,128)(2,1)} %kt_hbm.1, ...), custom_call_target="tpu_custom_call" | custom-call | tf_op jit(solution)/shard_map/joint_attention_step/pallas_call | solution.py:483
  43.9 0.6 %slice_bitcast_fusion = (f32[8,32]{1,0:T(8,128)}, f32[8,32]{1,0:T(8,128)}) fusion(f32[3,8,128]{2,1,0:T(8,128)S(1)} %joint_attention_step.1), kind=kLoop, calls=%fused_computation | loop fusion | bytes 4096 | tf_op jit(solution)/shard_map/squeeze | solution.py:530
  44.5 0.6 %slice.14 = f32[1,1,1]{2,1,0:T(1,128)} slice(f32[3,8,128]{2,1,0:T(8,128)S(1)} %joint_attention_step.1), slice={[2:3], [1:2], [32:33]} | slice | bytes 8 | tf_op jit(solution)/shard_map/slice | solution.py:531
  45.1 0.5 %slice.15 = f32[1,1,16]{2,1,0:T(1,128)} slice(f32[3,8,128]{2,1,0:T(8,128)S(1)} %joint_attention_step.1), slice={[2:3], [0:1], [0:16]} | slice | bytes 128 | tf_op jit(solution)/shard_map/slice | solution.py:532
